TPU v7x, 128 devices: a whole 4x4x4 slice. The times are simulated.
128 devices in a mesh: dp: 8 (over z, core), label: 16 (over x, y).
Axes of the slice: x: 4, y: 4, z: 4, core: 2. Of those that a mesh axis runs over, the one named last changes fastest.
Arguments:
- features: bfloat16 [262144, 768], P(('dp', 'label')), may hold values from -6 to 6
- inst_ids: int32 [2048, 4], P(('dp', 'label')), may hold values from 0 to 15
- lab_ids: int32 [2048, 4], P(('dp', 'label')), may hold values from 0 to 15
- counts: int32 [2048], P(('dp', 'label')), may hold values from 0 to 4, as said below
- block_bits: int32 [2048, 4, 128, 128], P(('dp', 'label')), may hold values 0 or 1
- centroids: bfloat16 [2048, 768], P('label'), may hold values from -40 to 40
Outputs:
- label_embed: bfloat16 [32768, 768], P(('dp', 'label'))
- membership: bfloat16 [32768, 2048], P(('dp', 'label'))
- targets: bfloat16 [262144, 768], P(('dp', 'label'))
Inputs may be any that keep to these rules, and one draw needn't show every extreme that they name: `lab_ids`: label block within the slot's label column. `counts`: in every draw one label column has all 4 slots used on every device.
All inputs are finite; a program needn't handle non-finite values. No bound on the sum of `block_bits` on one device may be relied on, other than what follows from the above.
Results may differ from a plain program's by a relative error of at most 0.008.
The roundings to bfloat16 on the way count: a program that leaves them out, or rounds other values in their place, can miss the bound.
Values may be sent and summed in bfloat16 or wider, within the bound.
No kernel may reach another device: no remote copies, remote signals or barrier semaphores. Data moves between devices by JAX's collectives and lax.ppermute only.
A program may use at most 128 MiB of HBM per device.

v0:
```python
import jax
import jax.numpy as jnp
from jax import lax
from jax.sharding import PartitionSpec as P

LB_DEV = 2
epsilon = 1e-05


def label_side(column_sums, centroids):
    embed32 = column_sums * lax.rsqrt(
        jnp.mean(column_sums * column_sums, axis=1, keepdims=True) + epsilon
    )
    label_embed = embed32.astype(jnp.bfloat16)
    all_rows = lax.all_gather(centroids, "label", axis=0, tiled=True)
    scores = jnp.einsum("rd,kd->rk", label_embed, all_rows, preferred_element_type=jnp.float32)
    row_peak = jnp.max(scores, axis=1, keepdims=True)
    lifted = jnp.exp(scores - row_peak)
    membership = (lifted / jnp.sum(lifted, axis=1, keepdims=True)).astype(jnp.bfloat16)
    mixed_rows = jnp.dot(membership, all_rows, preferred_element_type=jnp.float32)
    return (label_embed, membership, mixed_rows.astype(jnp.bfloat16))


def body(features, inst_ids, lab_ids, counts, block_bits, centroids):
    dest_count, slot_cap = inst_ids.shape
    block_size = block_bits.shape[-1]
    feat_width = features.shape[1]
    inst_blocks = features.reshape(-1, block_size, feat_width)
    gathered = inst_blocks[inst_ids]
    incidence = block_bits.astype(jnp.bfloat16)
    partials = jnp.einsum(
        "ncab,ncad->ncbd", incidence, gathered, preferred_element_type=jnp.float32
    ).astype(jnp.bfloat16)
    filled = jnp.arange(slot_cap)[None, :] < counts[:, None]
    tagged_ids = jnp.where(filled, lab_ids, -1)
    arrived, arrived_ids = (
        lax.all_to_all(partials, "label", split_axis=0, concat_axis=0, tiled=True),
        lax.all_to_all(tagged_ids, "label", split_axis=0, concat_axis=0, tiled=True),
    )
    share_rows = LB_DEV * block_size
    col_blocks = lax.axis_size("dp") * LB_DEV
    slot_total = dest_count * slot_cap
    flat_ids = arrived_ids.reshape(slot_total)
    selector = (flat_ids[None, :] == jnp.arange(col_blocks)[:, None]).astype(jnp.bfloat16)
    column_sums = jnp.dot(
        selector,
        arrived.reshape(slot_total, block_size * feat_width),
        preferred_element_type=jnp.float32,
    )
    column_total = lax.psum(column_sums, "dp")
    embed_all, member_all, column_mixed = label_side(
        column_total.reshape(col_blocks * block_size, feat_width), centroids
    )
    offset = lax.axis_index("dp") * share_rows
    label_embed = lax.dynamic_slice_in_dim(embed_all, offset, share_rows, 0)
    membership = lax.dynamic_slice_in_dim(member_all, offset, share_rows, 0)
    mixed_blocks = column_mixed.reshape(col_blocks, block_size, feat_width)
    picked = mixed_blocks[jnp.maximum(arrived_ids, 0)]
    picked = jnp.where((arrived_ids >= 0)[:, :, None, None], picked, jnp.zeros_like(picked))
    returned = lax.all_to_all(picked, "label", split_axis=0, concat_axis=0, tiled=True)
    contrib = jnp.einsum("ncab,ncbd->ncad", incidence, returned, preferred_element_type=jnp.float32)
    owner_map = (
        inst_ids.reshape(slot_total)[None, :] == jnp.arange(inst_blocks.shape[0])[:, None]
    ).astype(jnp.float32)
    raw_targets = jnp.dot(
        owner_map,
        contrib.reshape(slot_total, block_size * feat_width),
        precision=lax.Precision.HIGHEST,
    )
    raw_targets = raw_targets.reshape(-1, feat_width)
    targets = raw_targets * lax.rsqrt(
        jnp.mean(raw_targets * raw_targets, axis=1, keepdims=True) + epsilon
    )
    return (label_embed, membership, targets.astype(jnp.bfloat16))


def solution(mesh):
    in_specs = (
        P(("dp", "label"), None),
        P(("dp", "label"), None),
        P(("dp", "label"), None),
        P(("dp", "label")),
        P(("dp", "label"), None, None, None),
        P("label", None),
    )
    out_specs = (P(("dp", "label"), None), P(("dp", "label"), None), P(("dp", "label"), None))
    return jax.shard_map(body, mesh=mesh, in_specs=in_specs, out_specs=out_specs, check_vma=False)
```

profile of v0, /device:TPU:61, one launch (start us, length us, event | category | flops | bytes accessed | tf_op | source)
XLA Modules:
  0.0 778.2 jit_solution(7269517425034337055)
XLA Ops:
  8.0 0.8 select_bitcast_fusion
  9.5 6.6 all-to-all-start
  17.0 7.3 gather_fusion
  24.3 10.8 %convert_bitcast_fusion = bf16[16,4,128,768]{2,3,1,0:T(8,128)(2,1)} fusion(bf16[16,4,128,768]{3,2,1,0:T(8,128)(2,1)} %bitcast.31, s32[16,4,128,128]{3,2,1,0:T(8,128)} %param.10), kind=kOutput, calls=%fused_computation.5 | convolution fusion | flops 1617952768 | bytes 29360128 | tf_op jit(solution)/shard_map/ncab,ncad->ncbd/dot_general | solution.py:31
  35.1 6.7 all-to-all-start.1
  42.3 0.7 maximum_reduce_fusion
  43.1 219.6 %all-to-all-done.1 = bf16[16,4,128,768]{2,3,1,0:T(8,128)(2,1)} async-done(((bf16[16,4,128,768]{2,3,1,0:T(8,128)(2,1)}), bf16[16,4,128,768]{2,3,1,0:T(8,128)(2,1)}, u32[]{:S(2)}, u32[]{:S(2)}) %all-to-all-start.1) | async-done | bytes 12582944 | tf_op jit(solution)/shard_map/all_to_all | solution.py:37
  262.7 16.7 %copy.37 = bf16[8,8,128,768]{3,1,2,0:T(8,128)(2,1)} copy(bf16[8,8,128,768]{2,3,1,0:T(8,128)(2,1)} %bitcast.18) | data formatting | bytes 25165824
  279.4 9.0 %fusion.3 = f32[16,98304]{1,0:T(8,128)} fusion(bf16[64,98304]{1,0:T(8,128)(2,1)} %bitcast.34, s32[64]{0:T(128)S(1)} %eq.30), kind=kOutput, calls=%fused_computation.20 | convolution fusion | flops 201327616 | bytes 18874624 | tf_op jit(solution)/shard_map/dot_general | solution.py:45
  288.4 5.0 reshape.69
  294.3 91.9 %all-reduce.2.cloned.1.call-done = f32[2048,768]{1,0:T(8,128)} async-done(((f32[2048,768]{1,0:T(8,128)}), f32[2048,768]{1,0:T(8,128)}) %all-reduce.2.cloned.1.call-update) | async-done | bytes 6291472 | tf_op jit(solution)/shard_map/psum | solution.py:50
  386.2 3.4 multiply_reduce_fusion.1
  389.6 1.2 copy-done.3
  391.2 13.1 %fusion.7 = (f32[2048]{0:T(1024)S(1)}, f32[2048,2048]{0,1:T(8,128)}) fusion(bf16[2048,768]{1,0:T(8,128)(2,1)S(1)} %multiply_convert_fusion.1, bf16[2048,768]{1,0:T(8,128)(2,1)} %all-gather.2.cloned.1.call-done), kind=kOutput, calls=%fused_computation.32 | convolution fusion | flops 6446643200 | bytes 23076864 | tf_op jit(solution)/shard_map/rd,kd->rk/dot_general | solution.py:16
  404.4 8.1 %fusion = f32[2048]{0:T(1024)S(1)} fusion(f32[2048,2048]{0,1:T(8,128)} %get-tuple-element.15, f32[2048]{0:T(1024)S(1)} %get-tuple-element.14), kind=kLoop, calls=%fused_computation.4 | loop fusion | flops 8386560 | bytes 16793600 | tf_op jit(solution)/shard_map/reduce_sum | solution.py:19
  412.4 7.5 divide_convert_fusion
  419.9 7.3 convolution_convert_fusion
  427.3 7.1 gather_fusion.1
  434.4 16.6 %copy.34 = bf16[64,128,768]{1,2,0:T(8,128)(2,1)} copy(bf16[64,128,768]{2,1,0:T(8,128)(2,1)} %gather_fusion.1) | data formatting | bytes 25165824 | tf_op jit(solution)/shard_map/gather | solution.py:58
  451.0 10.6 %broadcast_select_fusion = bf16[16,4,128,768]{2,3,1,0:T(8,128)(2,1)} fusion(bf16[16,4,128,768]{2,3,1,0:T(8,128)(2,1)} %bitcast.32, pred[16,4]{1,0:T(8,128)(4,1)S(1)} %copy.33), kind=kLoop, calls=%fused_computation.6 | loop fusion | flops 6291456 | bytes 25165888 | tf_op jit(solution)/shard_map/jit(_where)/select_n | solution.py:59
  461.7 6.9 all-to-all-start.2
  468.7 1.3 constant_dynamic-slice_fusion
  470.0 1.4 copy.36
  471.4 1.8 constant_dynamic-slice_fusion.1
  473.2 232.2 %all-to-all-done.2 = bf16[16,4,128,768]{2,3,1,0:T(8,128)(2,1)} async-done(((bf16[16,4,128,768]{2,3,1,0:T(8,128)(2,1)}), bf16[16,4,128,768]{2,3,1,0:T(8,128)(2,1)}, u32[]{:S(2)}, u32[]{:S(2)}) %all-to-all-start.2) | async-done | bytes 12582944 | tf_op jit(solution)/shard_map/all_to_all | solution.py:60
  705.4 14.1 %convolution_bitcast_fusion = f32[16,4,128,768]{2,3,1,0:T(8,128)} fusion(bf16[16,4,128,768]{2,3,1,0:T(8,128)(2,1)} %all-to-all-done.2, s32[16,4,128,128]{3,2,1,0:T(8,128)} %param.10), kind=kOutput, calls=%fused_computation.7 | convolution fusion | flops 1611661312 | bytes 41943040 | tf_op jit(solution)/shard_map/ncab,ncbd->ncad/dot_general | solution.py:61
  719.5 25.1 %copy.38 = f32[8,8,128,768]{3,1,2,0:T(8,128)} copy(f32[8,8,128,768]{2,3,1,0:T(8,128)} %bitcast.29) | data formatting | bytes 50331648
  744.6 14.3 %fusion.4 = f32[16,98304]{1,0:T(8,128)} fusion(f32[64,98304]{1,0:T(8,128)} %bitcast.30, s32[64]{0:T(128)S(1)} %eq.34), kind=kOutput, calls=%fused_computation.21 | convolution fusion | flops 1207960576 | bytes 31457536 | tf_op jit(solution)/shard_map/dot_general | solution.py:65
  758.9 5.2 reshape.72
  764.1 3.4 multiply_reduce_fusion
  767.5 1.2 copy-done.2
  768.7 2.1 multiply_convert_fusion
  (37 shorter events, 3.7 us)
Async XLA Ops:
  8.0 9.0 %copy-start = (bf16[2048,768]{1,0:T(8,128)(2,1)S(1)}, bf16[2048,768]{1,0:T(8,128)(2,1)}, u32[]{:S(2)}) copy-start(bf16[2048,768]{1,0:T(8,128)(2,1)} %param.6) | copy-start | bytes 9437188
  9.5 25.5 %all-to-all-start = ((s32[16,1,4]{2,1,0:T(1,128)}), s32[16,1,4]{2,1,0:T(1,128)S(1)}, u32[]{:S(2)}, u32[]{:S(2)}) async-start(s32[16,1,4]{2,1,0:T(1,128)} %copy.27), calls=%async_computation | async-start | bytes 16384 | tf_op jit(solution)/shard_map/all_to_all | solution.py:38
  35.1 227.6 %all-to-all-start.1 = ((bf16[16,4,128,768]{2,3,1,0:T(8,128)(2,1)}), bf16[16,4,128,768]{2,3,1,0:T(8,128)(2,1)}, u32[]{:S(2)}, u32[]{:S(2)}) async-start(bf16[16,4,128,768]{2,3,1,0:T(8,128)(2,1)} %convert_bitcast_fusion), calls=%async_computation.1 | async-start | bytes 25165824 | tf_op jit(solution)/shard_map/all_to_all | solution.py:37
  41.7 344.4 %all-reduce.2.cloned.1.call-start = ((), (), s32[]{:S(2)}) async-start(), calls=%async_computation.3 | async-start | bytes 12582912 | tf_op jit(solution)/shard_map/psum | solution.py:50
  293.4 97.8 %all-gather.2.cloned.1.call-start = ((), (), s32[]{:S(2)}) async-start(), calls=%async_computation.4 | async-start | bytes 3342336 | tf_op jit(solution)/shard_map/all_gather | solution.py:15
  386.2 4.6 copy-start.3
  391.2 13.2 %copy-start.5 = (bf16[2048,768]{1,0:T(8,128)(2,1)}, bf16[2048,768]{1,0:T(8,128)(2,1)S(1)}, u32[]{:S(2)}) copy-start(bf16[2048,768]{1,0:T(8,128)(2,1)S(1)} %multiply_convert_fusion.1) | copy-start | bytes 9437188
  412.4 7.5 copy-start.7
  419.9 7.3 copy-start.4
  461.7 6.9 copy-start.6
  461.7 243.7 %all-to-all-start.2 = ((bf16[16,4,128,768]{2,3,1,0:T(8,128)(2,1)}), bf16[16,4,128,768]{2,3,1,0:T(8,128)(2,1)}, u32[]{:S(2)}, u32[]{:S(2)}) async-start(bf16[16,4,128,768]{2,3,1,0:T(8,128)(2,1)} %broadcast_select_fusion), calls=%async_computation.2 | async-start | bytes 25165824 | tf_op jit(solution)/shard_map/all_to_all | solution.py:60
  758.9 11.8 %copy-start.1 = (bf16[2048,768]{1,0:T(8,128)(2,1)S(1)}, bf16[2048,768]{1,0:T(8,128)(2,1)}, u32[]{:S(2)}) copy-start(bf16[2048,768]{1,0:T(8,128)(2,1)} %param.6) | copy-start | bytes 9437188
  764.1 4.6 copy-start.2
Sparse Core Ops, SparseCore 0:
  293.5 92.5 all-reduce.1
Sparse Core Ops, SparseCore 1:
  296.1 53.1 all-gather.1
where the time goes:
time: 780 us; the launch traced here: 778 us
  waiting for transfers between devices  544 us (70%)
  local copies, waits for them, and re-layouts  91.8 us (12%)
  matrix products  68.7 us (9%)
  other arithmetic  37.7 us (5%)
  starting transfers between devices  20.2 us (3%)
  between operations  15.6 us (2%)
    all_to_all x1, waiting for transfers between devices, body(): lax.all_to_all(picked, 'label', split_axis=0, concat_axis=0, tiled=True)  232 us
    all_to_all x1, waiting for transfers between devices, body(): lax.all_to_all(partials, 'label', split_axis=0, concat_axis=0, tiled=True)  220 us
    psum x1, waiting for transfers between devices, body(): column_total = lax.psum(column_sums, 'dp')  91.9 us
    unnamed x20, local copies, waits for them, and re-layouts  45.7 us
    gather x2, local copies, waits for them, and re-layouts, body(): picked = mixed_blocks[jnp.maximum(arrived_ids, 0)]  23.8 us
  transfers between devices with their start and end apart: 5, of which 3 were waited for; matrix products, arithmetic and copies ran while one was open for 4% of the time, Pallas kernels for 0%

commit v1 on v0

--- a/solution.py
+++ b/solution.py
@@ -1,3 +1,4 @@
+import functools
 import jax
 import jax.numpy as jnp
 from jax import lax
@@ -5,6 +6,20 @@
 
 LB_DEV = 2
 epsilon = 1e-05
+
+
+def outputs_move(piece_in, bus_axis):
+    degree = lax.axis_size(bus_axis)
+    current_arr = lambda frame_out: [(no, no ^ frame_out) for no in range(degree)]
+    a_next = piece_in
+    for q in range(degree.bit_length() - 1):
+        b_next = current_arr(1 << q)
+        tall = lax.ppermute(a_next, bus_axis, perm=b_next)
+        a_next = a_next + tall
+    return a_next
+
+
+open_the_plane = functools.partial(outputs_move, bus_axis="dp")
 
 
 def label_side(column_sums, centroids):
@@ -47,7 +62,7 @@
         arrived.reshape(slot_total, block_size * feat_width),
         preferred_element_type=jnp.float32,
     )
-    column_total = lax.psum(column_sums, "dp")
+    column_total = open_the_plane(column_sums)
     embed_all, member_all, column_mixed = label_side(
         column_total.reshape(col_blocks * block_size, feat_width), centroids
     )

time: 780 us -> 977 us (1.25)
  waiting for transfers between devices: 544 us -> 713 us
  other arithmetic: 37.7 us -> 52.5 us
  starting transfers between devices: 20.2 us -> 30.6 us
    ppermute x0 -> x3, waiting for transfers between devices: none -> 281 us  [outputs_move(): tall = lax.ppermute(a_next, bus_axis, perm=b_next)]
    psum x1 -> x0, waiting for transfers between devices: 91.9 us -> none  [body(): column_total = lax.psum(column_sums, 'dp')]
    all_to_all x1, waiting for transfers between devices: 232 us -> 212 us  [body(): lax.all_to_all(picked, 'label', split_axis=0, concat_axis=0, tiled=True)]
    add x0 -> x3, other arithmetic: none -> 14.7 us  [outputs_move(): a_next = a_next + tall]
  transfers between devices with their start and end apart: 5 -> 7, of which waited for: 3 -> 5; matrix products, arithmetic and copies ran while one was open for 4% -> 4% of each run, Pallas kernels for 0% -> 0%
where the time goes in v1:
time: 977 us; the launch traced here: 967 us
  waiting for transfers between devices  713 us (73%)
  local copies, waits for them, and re-layouts  91.9 us (9%)
  matrix products  65.3 us (7%)
  other arithmetic  52.5 us (5%)
  starting transfers between devices  30.6 us (3%)
  between operations  14.2 us (1%)
    ppermute x3, waiting for transfers between devices, outputs_move(): tall = lax.ppermute(a_next, bus_axis, perm=b_next)  281 us
    all_to_all x1, waiting for transfers between devices, body(): lax.all_to_all(partials, 'label', split_axis=0, concat_axis=0, tiled=True)  220 us
    all_to_all x1, waiting for transfers between devices, body(): lax.all_to_all(picked, 'label', split_axis=0, concat_axis=0, tiled=True)  212 us
    unnamed x20, local copies, waits for them, and re-layouts  45.7 us
    gather x2, local copies, waits for them, and re-layouts, body(): picked = mixed_blocks[jnp.maximum(arrived_ids, 0)]  24 us
  transfers between devices with their start and end apart: 7, of which 5 were waited for; matrix products, arithmetic and copies ran while one was open for 4% of the time, Pallas kernels for 0%

profile of v1, /device:TPU:61, one launch (start us, length us, event | category | flops | bytes accessed | tf_op | source)
XLA Modules:
  0.0 967.1 jit_solution(12363704185281337248)
XLA Ops:
  8.7 6.6 all-to-all-start
  16.1 7.3 gather_fusion
  23.4 10.7 %convert_bitcast_fusion = bf16[16,4,128,768]{2,3,1,0:T(8,128)(2,1)} fusion(bf16[16,4,128,768]{3,2,1,0:T(8,128)(2,1)} %bitcast.31, s32[16,4,128,128]{3,2,1,0:T(8,128)} %param.10), kind=kOutput, calls=%fused_computation.5 | convolution fusion | flops 1617952768 | bytes 29360128 | tf_op jit(solution)/shard_map/ncab,ncad->ncbd/dot_general | solution.py:46
  34.1 6.7 all-to-all-start.1
  42.1 219.5 %all-to-all-done.1 = bf16[16,4,128,768]{2,3,1,0:T(8,128)(2,1)} async-done(((bf16[16,4,128,768]{2,3,1,0:T(8,128)(2,1)}), bf16[16,4,128,768]{2,3,1,0:T(8,128)(2,1)}, u32[]{:S(2)}, u32[]{:S(2)}) %all-to-all-start.1) | async-done | bytes 12582944 | tf_op jit(solution)/shard_map/all_to_all | solution.py:52
  261.7 16.7 %copy.37 = bf16[8,8,128,768]{3,1,2,0:T(8,128)(2,1)} copy(bf16[8,8,128,768]{2,3,1,0:T(8,128)(2,1)} %bitcast.18) | data formatting | bytes 25165824
  278.4 5.6 fusion.3
  284.0 2.3 collective-permute-start
  286.3 9.9 %collective-permute-done = f32[16,98304]{1,0:T(8,128)} collective-permute-done((f32[16,98304]{1,0:T(8,128)S(1)}, f32[16,98304]{1,0:T(8,128)}, u32[]{:S(2)}, u32[]{:S(2)}) %collective-permute-start) | collective-permute-done | bytes 6291488 | tf_op jit(solution)/shard_map/ppermute | solution.py:17
  296.2 3.6 add.34
  299.8 136.7 %collective-permute-done.1 = f32[16,98304]{1,0:T(8,128)S(1)} collective-permute-done((f32[16,98304]{1,0:T(8,128)S(1)}, f32[16,98304]{1,0:T(8,128)S(1)}, u32[]{:S(2)}, u32[]{:S(2)}) %collective-permute-start.1) | collective-permute-done | bytes 6291488 | tf_op jit(solution)/shard_map/ppermute | solution.py:17
  436.5 3.3 add.35
  439.8 2.8 collective-permute-start.2
  442.9 134.6 %collective-permute-done.2 = f32[16,98304]{1,0:T(8,128)} collective-permute-done((f32[16,98304]{1,0:T(8,128)}, f32[16,98304]{1,0:T(8,128)}, u32[]{:S(2)}, u32[]{:S(2)}) %collective-permute-start.2) | collective-permute-done | bytes 6291488 | tf_op jit(solution)/shard_map/ppermute | solution.py:17
  577.5 7.9 add.36
  585.3 5.0 reshape.69
  590.3 3.4 multiply_reduce_fusion.1
  595.4 13.3 %fusion.7 = (f32[2048]{0:T(1024)S(1)}, f32[2048,2048]{0,1:T(8,128)}) fusion(bf16[2048,768]{1,0:T(8,128)(2,1)S(1)} %multiply_convert_fusion.1, bf16[2048,768]{1,0:T(8,128)(2,1)} %all-gather.2.cloned.1.call-done), kind=kOutput, calls=%fused_computation.32 | convolution fusion | flops 6446643200 | bytes 23076864 | tf_op jit(solution)/shard_map/rd,kd->rk/dot_general | solution.py:31
  608.7 8.1 fusion
  616.7 7.5 divide_convert_fusion
  624.2 7.3 convolution_convert_fusion
  631.6 7.3 gather_fusion.1
  638.9 16.7 %copy.34 = bf16[64,128,768]{1,2,0:T(8,128)(2,1)} copy(bf16[64,128,768]{2,1,0:T(8,128)(2,1)} %gather_fusion.1) | data formatting | bytes 25165824 | tf_op jit(solution)/shard_map/gather | solution.py:73
  655.6 10.7 %broadcast_select_fusion = bf16[16,4,128,768]{2,3,1,0:T(8,128)(2,1)} fusion(bf16[16,4,128,768]{2,3,1,0:T(8,128)(2,1)} %bitcast.32, pred[16,4]{1,0:T(8,128)(4,1)S(1)} %copy.33), kind=kLoop, calls=%fused_computation.6 | loop fusion | flops 6291456 | bytes 25165888 | tf_op jit(solution)/shard_map/jit(_where)/select_n | solution.py:74
  666.3 12.2 %all-to-all-start.2 = ((bf16[16,4,128,768]{2,3,1,0:T(8,128)(2,1)}), bf16[16,4,128,768]{2,3,1,0:T(8,128)(2,1)}, u32[]{:S(2)}, u32[]{:S(2)}) async-start(bf16[16,4,128,768]{2,3,1,0:T(8,128)(2,1)} %broadcast_select_fusion), calls=%async_computation.2 | async-start | bytes 25165824 | tf_op jit(solution)/shard_map/all_to_all | solution.py:75
  683.2 211.8 %all-to-all-done.2 = bf16[16,4,128,768]{2,3,1,0:T(8,128)(2,1)} async-done(((bf16[16,4,128,768]{2,3,1,0:T(8,128)(2,1)}), bf16[16,4,128,768]{2,3,1,0:T(8,128)(2,1)}, u32[]{:S(2)}, u32[]{:S(2)}) %all-to-all-start.2) | async-done | bytes 12582944 | tf_op jit(solution)/shard_map/all_to_all | solution.py:75
  895.0 14.1 %convolution_bitcast_fusion = f32[16,4,128,768]{2,3,1,0:T(8,128)} fusion(bf16[16,4,128,768]{2,3,1,0:T(8,128)(2,1)} %all-to-all-done.2, s32[16,4,128,128]{3,2,1,0:T(8,128)} %param.10), kind=kOutput, calls=%fused_computation.7 | convolution fusion | flops 1611661312 | bytes 41943040 | tf_op jit(solution)/shard_map/ncab,ncbd->ncad/dot_general | solution.py:76
  909.1 25.1 %copy.38 = f32[8,8,128,768]{3,1,2,0:T(8,128)} copy(f32[8,8,128,768]{2,3,1,0:T(8,128)} %bitcast.29) | data formatting | bytes 50331648
  934.3 14.3 %fusion.4 = f32[16,98304]{1,0:T(8,128)} fusion(f32[64,98304]{1,0:T(8,128)} %bitcast.30, s32[64]{0:T(128)S(1)} %eq.34), kind=kOutput, calls=%fused_computation.21 | convolution fusion | flops 1207960576 | bytes 31457536 | tf_op jit(solution)/shard_map/dot_general | solution.py:80
  948.6 5.0 reshape.72
  953.6 3.4 multiply_reduce_fusion
  958.2 2.1 multiply_convert_fusion
  (43 shorter events, 11.6 us)
Async XLA Ops:
  7.2 9.0 copy-start
  8.7 25.4 %all-to-all-start = ((s32[16,1,4]{2,1,0:T(1,128)}), s32[16,1,4]{2,1,0:T(1,128)S(1)}, u32[]{:S(2)}, u32[]{:S(2)}) async-start(s32[16,1,4]{2,1,0:T(1,128)} %copy.27), calls=%async_computation | async-start | bytes 16384 | tf_op jit(solution)/shard_map/all_to_all | solution.py:53
  34.1 227.5 %all-to-all-start.1 = ((bf16[16,4,128,768]{2,3,1,0:T(8,128)(2,1)}), bf16[16,4,128,768]{2,3,1,0:T(8,128)(2,1)}, u32[]{:S(2)}, u32[]{:S(2)}) async-start(bf16[16,4,128,768]{2,3,1,0:T(8,128)(2,1)} %convert_bitcast_fusion), calls=%async_computation.1 | async-start | bytes 25165824 | tf_op jit(solution)/shard_map/all_to_all | solution.py:52
  40.8 554.6 %all-gather.2.cloned.1.call-start = ((), (), s32[]{:S(2)}) async-start(), calls=%async_computation.3 | async-start | bytes 3342336 | tf_op jit(solution)/shard_map/all_gather | solution.py:30
  284.0 12.2 %collective-permute-start = (f32[16,98304]{1,0:T(8,128)S(1)}, f32[16,98304]{1,0:T(8,128)}, u32[]{:S(2)}, u32[]{:S(2)}) collective-permute-start(f32[16,98304]{1,0:T(8,128)S(1)} %fusion.3), channel_id=1, source_target_pairs={{0,16},{16,0},{32,48},{48,32},{64,80},{80,64},{96,112},{112,96},{1... | collective-permute-start | bytes 18874376 | tf_op jit(solution)/shard_map/ppermute | solution.py:17
  299.7 136.8 %collective-permute-start.1 = (f32[16,98304]{1,0:T(8,128)S(1)}, f32[16,98304]{1,0:T(8,128)S(1)}, u32[]{:S(2)}, u32[]{:S(2)}) collective-permute-start(f32[16,98304]{1,0:T(8,128)S(1)} %add.34), channel_id=1, source_target_pairs={{0,32},{16,48},{32,0},{48,16},{64,96},{80,112},{96,64},{112,80},{1... | collective-permute-start | bytes 18874376 | tf_op jit(solution)/shard_map/ppermute | solution.py:17
  439.8 137.7 %collective-permute-start.2 = (f32[16,98304]{1,0:T(8,128)}, f32[16,98304]{1,0:T(8,128)}, u32[]{:S(2)}, u32[]{:S(2)}) collective-permute-start(f32[16,98304]{1,0:T(8,128)} %add.35), channel_id=1, source_target_pairs={{0,64},{16,80},{32,96},{48,112},{64,0},{80,16},{96,32},{112,48},{1... | collective-permute-start | bytes 18874376 | tf_op jit(solution)/shard_map/ppermute | solution.py:17
  590.3 4.6 copy-start.2
  595.3 13.3 %copy-start.5 = (bf16[2048,768]{1,0:T(8,128)(2,1)}, bf16[2048,768]{1,0:T(8,128)(2,1)S(1)}, u32[]{:S(2)}) copy-start(bf16[2048,768]{1,0:T(8,128)(2,1)S(1)} %multiply_convert_fusion.1) | copy-start | bytes 9437188
  616.7 7.5 copy-start.7
  624.2 7.3 copy-start.4
  666.3 12.2 %copy-start.6 = (s32[16,4]{0,1:T(4,128)S(1)}, s32[16,4]{0,1:T(4,128)}, u32[]{:S(2)}) copy-start(s32[16,4]{0,1:T(4,128)} %param.7) | copy-start | bytes 772
  666.3 228.7 %all-to-all-start.2 = ((bf16[16,4,128,768]{2,3,1,0:T(8,128)(2,1)}), bf16[16,4,128,768]{2,3,1,0:T(8,128)(2,1)}, u32[]{:S(2)}, u32[]{:S(2)}) async-start(bf16[16,4,128,768]{2,3,1,0:T(8,128)(2,1)} %broadcast_select_fusion), calls=%async_computation.2 | async-start | bytes 25165824 | tf_op jit(solution)/shard_map/all_to_all | solution.py:75
  953.6 4.6 copy-start.3
  953.6 6.7 copy-start.1
Sparse Core Ops, SparseCore 0:
  442.7 50.6 all-gather.1
